TPU v7x, 128 devices: a whole 4x4x4 slice. The times are simulated.
128 devices in a mesh: region: 16 (over y, x_hi, core), ctx: 8 (over z, x_lo).
Axes of the slice: x: 4 (x_hi: 2, x_lo: 2; x = x_hi * 2 + x_lo), y: 4, z: 4, core: 2. Of those that a mesh axis runs over, the one named last changes fastest.
Arguments:
- tokens: bfloat16 [16, 4096, 1152], P('region', 'ctx'), may hold values from -6 to 6
- element_ids: int32 [16, 4096], P('region', 'ctx'), may hold values from 0 to 16383, as said below
- element_slot: int32 [16384], replicated, may hold values from 0 to 16383, as said below
- live_count: int32 [16, 8], P('region', 'ctx'), may hold values from 128 to 512
- cond_table: bfloat16 [16384, 1152], P(('region', 'ctx')), may hold values from -6 to 6
- w_ada: bfloat16 [1152, 3456], replicated, may hold values from -0.1875 to 0.1875
- b_ada: float32 [3456], replicated, may hold values from -3 to 3
- w_qkv: bfloat16 [1152, 3456], replicated, may hold values from -8 to 8
- w_out: bfloat16 [1152, 1152], replicated, may hold values from -0.1875 to 0.1875
Outputs:
- block_out: bfloat16 [16, 4096, 1152], P('region', 'ctx')
Inputs may be any that keep to these rules, and one draw needn't show every extreme that they name: element_ids: within each device's block of 512 patches (region r, positions c * 512 to (c + 1) * 512 - 1, device r * 8 + c of region+ctx), at most 6 patches name elements whose table row lies on one device (rows o * 128 to (o + 1) * 128 - 1); in every block some device is named by exactly 6 solid patches. element_slot is a permutation: element e is row element_slot[e] of cond_table.
All inputs are finite; a program needn't handle non-finite values.
Results may differ from a plain program's by a relative error of at most 0.027.
Values may be sent and summed in bfloat16 or wider, within the bound.
A program may use at most 192 MiB of HBM per device.

v0:
```python
import math
import jax
import jax.numpy as jnp
from jax import lax
from jax.sharding import PartitionSpec as P

HEADS = 16


def layer_modulate(device_tokens, mods, width):
    values = device_tokens.astype(jnp.float32)
    center = jnp.mean(values, axis=1, keepdims=True)
    spread = jnp.mean((values - center) ** 2, axis=1, keepdims=True)
    normed = (values - center) * lax.rsqrt(spread + 1e-06)
    shift = mods[:, :width]
    scale = mods[:, width : 2 * width]
    return (normed * (1.0 + scale) + shift).astype(jnp.bfloat16)


def per_device(
    tokens, element_ids, element_slot, live_count, cond_table, w_ada, b_ada, w_qkv, w_out
):
    device_tokens = tokens[0]
    tok_rows, width = device_tokens.shape
    owners = lax.axis_size(("region", "ctx"))
    elem_rows = cond_table.shape[0]
    capacity = max(2, 3 * tok_rows // (2 * owners))
    slots = element_slot[element_ids[0]]
    owner_index = slots // elem_rows
    local_row = slots % elem_rows
    position = jnp.arange(tok_rows, dtype=jnp.int32)
    solid = position < live_count[0, 0]
    earlier = (
        (owner_index[:, None] == owner_index[None, :])
        & (position[None, :] < position[:, None])
        & solid[None, :]
    )
    place_rank = jnp.sum(earlier.astype(jnp.int32), axis=1)
    target = jnp.where(solid, owner_index * capacity + place_rank, owners * capacity)
    requests = jnp.zeros((owners * capacity,), jnp.int32).at[target].set(local_row, mode="drop")
    asked = lax.all_to_all(
        requests.reshape(owners, capacity),
        ("region", "ctx"),
        split_axis=0,
        concat_axis=0,
        tiled=True,
    ).reshape(-1)
    pick_at = jnp.minimum(target, owners * capacity - 1)
    served = cond_table[asked].reshape(owners, capacity, width)
    replies = lax.all_to_all(served, ("region", "ctx"), split_axis=0, concat_axis=0, tiled=True)
    picked = replies.reshape(owners * capacity, width)[pick_at]
    activated = jnp.where(solid[:, None], jax.nn.silu(picked.astype(jnp.float32)), 0.0).astype(
        jnp.bfloat16
    )
    mods = (jnp.dot(activated, w_ada, preferred_element_type=jnp.float32) + b_ada).astype(
        jnp.bfloat16
    )
    mods = mods.astype(jnp.float32)
    modulated = layer_modulate(device_tokens, mods, width)
    qkv = jnp.dot(modulated, w_qkv, preferred_element_type=jnp.float32).astype(jnp.bfloat16)
    queries = qkv[:, :width]
    keys_here = qkv[:, width : 2 * width]
    values_here = qkv[:, 2 * width :]
    head_dim = width // HEADS
    inverse_root = 1.0 / math.sqrt(head_dim)
    query_heads = queries.reshape(tok_rows, HEADS, head_dim)
    initial = (
        jnp.full((HEADS, tok_rows), -1e30, jnp.float32),
        jnp.zeros((HEADS, tok_rows), jnp.float32),
        jnp.zeros((HEADS, tok_rows, head_dim), jnp.float32),
    )
    keys_piece = lax.all_gather(keys_here, "ctx", axis=0, tiled=True)
    values_piece = lax.all_gather(values_here, "ctx", axis=0, tiled=True)
    piece_rows = keys_piece.shape[0]
    block_rows = math.gcd(piece_rows, 512)
    key_blocks = keys_piece.reshape(piece_rows // block_rows, block_rows, HEADS, head_dim)
    value_blocks = values_piece.reshape(piece_rows // block_rows, block_rows, HEADS, head_dim)

    def advance(state, blocks):
        running_max, denominator, weighted = state
        key_block, value_block = blocks
        scores = (
            jnp.einsum("qhe,khe->hqk", query_heads, key_block, preferred_element_type=jnp.float32)
            * inverse_root
        )
        new_max = jnp.maximum(running_max, jnp.max(scores, axis=2))
        shrink = jnp.exp(running_max - new_max)
        expo = jnp.exp(scores - new_max[:, :, None])
        denominator = denominator * shrink + jnp.sum(expo, axis=2)
        weighted = weighted * shrink[:, :, None] + jnp.einsum(
            "hqk,khe->hqe",
            expo.astype(jnp.bfloat16),
            value_block,
            preferred_element_type=jnp.float32,
        )
        return ((new_max, denominator, weighted), None)

    result, _ = lax.scan(advance, initial, (key_blocks, value_blocks))
    final_max, denominator, weighted = result
    result = weighted / denominator[:, :, None]
    attended = jnp.transpose(result, (1, 0, 2)).reshape(tok_rows, width).astype(jnp.bfloat16)
    projected = jnp.dot(attended, w_out, preferred_element_type=jnp.float32)
    gate = mods[:, 2 * width :]
    output = (device_tokens.astype(jnp.float32) + gate * projected).astype(jnp.bfloat16)
    return output[None]


def solution(mesh):
    placed = (
        P("region", "ctx", None),
        P("region", "ctx"),
        P(),
        P("region", "ctx"),
        P(("region", "ctx"), None),
        P(),
        P(),
        P(),
        P(),
    )
    return jax.shard_map(
        per_device, mesh=mesh, in_specs=placed, out_specs=P("region", "ctx", None), check_vma=False
    )
```

profile of v0, /device:TPU:1, one launch (start us, length us, event | category | flops | bytes accessed | tf_op | source)
XLA Modules:
  0.0 791.2 jit_solution(2168846437949532841)
XLA Ops:
  14.5 21.0 %all_to_all.14 = s32[128,1,6]{2,1,0:T(1,128)S(1)} all-to-all(s32[128,1,6]{2,1,0:T(1,128)S(1)} %bitcast.77), channel_id=1, replica_groups=mesh['region'=16,'ctx'=8] {'region','ctx'}, dimensions={0} | all-to-all | bytes 6144 | tf_op jit(solution)/shard_map/all_to_all | solution.py:41
  53.4 29.6 %all-to-all-done.1 = bf16[128,6,1152]{2,1,0:T(8,128)(2,1)} async-done(((bf16[128,6,1152]{2,1,0:T(8,128)(2,1)}), bf16[128,6,1152]{2,1,0:T(8,128)(2,1)}, u32[]{:S(2)}, u32[]{:S(2)}) %all-to-all-start.1) | async-done | bytes 1769504 | tf_op jit(solution)/shard_map/all_to_all | solution.py:50
  100.3 11.4 %convolution_convert_fusion = bf16[512,3456]{1,0:T(8,128)(2,1)S(1)} fusion(bf16[1152,3456]{1,0:T(8,128)(2,1)} %param.18, bf16[1,512,1152]{2,1,0:T(8,128)(2,1)S(1)} %copy-done.2, f32[512,3456]{1,0:T(8,128)S(1)} %fusion.19, f32[512]{0:T(512)S(1)} %add_rsqrt_fusion, f32[512]{0:T(512)S(1)} %broadcast_multiply_fusion), kind=kOutput, calls=%fused_computation.28 | convolution fusion | flops 4082761728 | bytes 17403904 | tf_op jit(solution)/shard_map/dot_general | solution.py:60
  116.9 180.6 %all-gather.3.cloned.1.call-done = bf16[4096,1152]{1,0:T(8,128)(2,1)} async-done(((bf16[512,1152]{1,0:T(8,128)(2,1)}), bf16[4096,1152]{1,0:T(8,128)(2,1)}) %all-gather.3.cloned.1.call-update) | async-done | bytes 9437200 | tf_op jit(solution)/shard_map/all_gather | solution.py:72
  297.5 33.2 %reshape.260 = bf16[8,512,16,72]{3,2,1,0:T(8,128)(2,1)} reshape(bf16[4096,1152]{1,0:T(8,128)(2,1)} %all-gather.3.cloned.1.call-done) | data formatting | bytes 18874368 | tf_op jit(solution)/shard_map/reshape | solution.py:76
  330.7 21.5 %copy.32 = bf16[8,512,16,72]{1,3,2,0:T(8,128)(2,1)} copy(bf16[8,512,16,72]{3,2,1,0:T(8,128)(2,1)} %reshape.260) | data formatting | bytes 18874368
  352.2 136.0 %all-gather.5.cloned.1.call-done = bf16[4096,1152]{1,0:T(8,128)(2,1)} async-done(((bf16[512,1152]{1,0:T(8,128)(2,1)}), bf16[4096,1152]{1,0:T(8,128)(2,1)}) %all-gather.5.cloned.1.call-update) | async-done | bytes 9437200 | tf_op jit(solution)/shard_map/all_gather | solution.py:73
  488.2 33.2 %reshape.261 = bf16[8,512,16,72]{3,2,1,0:T(8,128)(2,1)} reshape(bf16[4096,1152]{1,0:T(8,128)(2,1)} %all-gather.5.cloned.1.call-done) | data formatting | bytes 18874368 | tf_op jit(solution)/shard_map/reshape | solution.py:77
  521.4 21.4 %copy.33 = bf16[8,512,16,72]{1,3,2,0:T(8,128)(2,1)} copy(bf16[8,512,16,72]{3,2,1,0:T(8,128)(2,1)} %reshape.261) | data formatting | bytes 18874368
  542.9 234.7 %while.15 = (s32[]{:T(128)}, f32[16,512]{1,0:T(8,128)S(1)}, f32[16,512]{1,0:T(8,128)S(1)}, f32[16,512,72]{1,2,0:T(8,128)}, bf16[8,512,16,72]{1,3,2,0:T(8,128)(2,...) while((s32[]{:T(128)}, f32[16,512]{1,0:T(8,128)S(1)}, ...), condition=%wide.region_7.8_spmd.clone, body=%wide.region_4.7_spmd.clone.sunk | while | flops 1243324416 | bytes 59114596 | solution.py:98
  542.9 9.7 %bitcast_reduce_fusion.2 = (f32[16,512]{1,0:T(8,128)S(1)}, f32[16,512,512]{2,1,0:T(8,128)}) fusion(bf16[512,16,72]{0,2,1:T(8,128)(2,1)} %get-tuple-element.196, bf16[8,512,16,72]{1,3,2,0:T(8,128)(2,1)} %get-tuple-element.195, s32[]{:T(128)} %get-tuple-element.182), kind=kOutput, calls=%fused_computation.5.clone.1 | convolution fusion | flops 612360192 | bytes 19169792 | tf_op jit(solution)/shard_map/while/body/eval_jaxpr/qhe,khe->hqk/dot_general | solution.py:83
  552.6 8.6 %fusion.67 = f32[16,512]{1,0:T(8,128)S(1)} fusion(f32[16,512,512]{2,1,0:T(8,128)} %get-tuple-element.170, f32[16,512]{1,0:T(8,128)S(1)} %select_maximum_fusion.2), kind=kLoop, calls=%fused_computation.8.clone.1 | loop fusion | flops 12574720 | bytes 16842752 | tf_op jit(solution)/shard_map/while/body/eval_jaxpr/reduce_sum | solution.py:89
  561.2 10.4 %fusion.69 = f32[16,512,72]{1,2,0:T(8,128)} fusion(f32[16,512,72]{1,2,0:T(8,128)} %get-tuple-element.185, f32[16,512,512]{2,1,0:T(8,128)} %get-tuple-element.170, f32[16,512]{1,0:T(8,128)S(1)} %select_maximum_fusion.2, bf16[8,512,16,72]{1,3,2,0:T(8,128)(2,1)} %get-tuple-element.197, s32[]{:T(128)} %get-tuple-element.182, ...), kind=kOutput, calls=%fused_computation.13.clone.1 | convolution fusion | flops 618332160 | bytes 22741504 | tf_op jit(solution)/shard_map/while/body/eval_jaxpr/hqk,khe->hqe/dot_general | solution.py:90
  571.6 9.7 %bitcast_reduce_fusion.2 = (f32[16,512]{1,0:T(8,128)S(1)}, f32[16,512,512]{2,1,0:T(8,128)}) fusion(bf16[512,16,72]{0,2,1:T(8,128)(2,1)} %get-tuple-element.196, bf16[8,512,16,72]{1,3,2,0:T(8,128)(2,1)} %get-tuple-element.195, s32[]{:T(128)} %get-tuple-element.182), kind=kOutput, calls=%fused_computation.5.clone.1 | convolution fusion | flops 612360192 | bytes 19169792 | tf_op jit(solution)/shard_map/while/body/eval_jaxpr/qhe,khe->hqk/dot_general | solution.py:83
  581.3 8.6 %fusion.67 = f32[16,512]{1,0:T(8,128)S(1)} fusion(f32[16,512,512]{2,1,0:T(8,128)} %get-tuple-element.170, f32[16,512]{1,0:T(8,128)S(1)} %select_maximum_fusion.2), kind=kLoop, calls=%fused_computation.8.clone.1 | loop fusion | flops 12574720 | bytes 16842752 | tf_op jit(solution)/shard_map/while/body/eval_jaxpr/reduce_sum | solution.py:89
  589.9 11.1 %fusion.69 = f32[16,512,72]{1,2,0:T(8,128)} fusion(f32[16,512,72]{1,2,0:T(8,128)} %get-tuple-element.185, f32[16,512,512]{2,1,0:T(8,128)} %get-tuple-element.170, f32[16,512]{1,0:T(8,128)S(1)} %select_maximum_fusion.2, bf16[8,512,16,72]{1,3,2,0:T(8,128)(2,1)} %get-tuple-element.197, s32[]{:T(128)} %get-tuple-element.182, ...), kind=kOutput, calls=%fused_computation.13.clone.1 | convolution fusion | flops 618332160 | bytes 22741504 | tf_op jit(solution)/shard_map/while/body/eval_jaxpr/hqk,khe->hqe/dot_general | solution.py:90
  601.0 9.7 %bitcast_reduce_fusion.2 = (f32[16,512]{1,0:T(8,128)S(1)}, f32[16,512,512]{2,1,0:T(8,128)}) fusion(bf16[512,16,72]{0,2,1:T(8,128)(2,1)} %get-tuple-element.196, bf16[8,512,16,72]{1,3,2,0:T(8,128)(2,1)} %get-tuple-element.195, s32[]{:T(128)} %get-tuple-element.182), kind=kOutput, calls=%fused_computation.5.clone.1 | convolution fusion | flops 612360192 | bytes 19169792 | tf_op jit(solution)/shard_map/while/body/eval_jaxpr/qhe,khe->hqk/dot_general | solution.py:83
  619.3 11.1 %fusion.69 = f32[16,512,72]{1,2,0:T(8,128)} fusion(f32[16,512,72]{1,2,0:T(8,128)} %get-tuple-element.185, f32[16,512,512]{2,1,0:T(8,128)} %get-tuple-element.170, f32[16,512]{1,0:T(8,128)S(1)} %select_maximum_fusion.2, bf16[8,512,16,72]{1,3,2,0:T(8,128)(2,1)} %get-tuple-element.197, s32[]{:T(128)} %get-tuple-element.182, ...), kind=kOutput, calls=%fused_computation.13.clone.1 | convolution fusion | flops 618332160 | bytes 22741504 | tf_op jit(solution)/shard_map/while/body/eval_jaxpr/hqk,khe->hqe/dot_general | solution.py:90
  630.4 9.7 %bitcast_reduce_fusion.2 = (f32[16,512]{1,0:T(8,128)S(1)}, f32[16,512,512]{2,1,0:T(8,128)}) fusion(bf16[512,16,72]{0,2,1:T(8,128)(2,1)} %get-tuple-element.196, bf16[8,512,16,72]{1,3,2,0:T(8,128)(2,1)} %get-tuple-element.195, s32[]{:T(128)} %get-tuple-element.182), kind=kOutput, calls=%fused_computation.5.clone.1 | convolution fusion | flops 612360192 | bytes 19169792 | tf_op jit(solution)/shard_map/while/body/eval_jaxpr/qhe,khe->hqk/dot_general | solution.py:83
  640.2 8.6 %fusion.67 = f32[16,512]{1,0:T(8,128)S(1)} fusion(f32[16,512,512]{2,1,0:T(8,128)} %get-tuple-element.170, f32[16,512]{1,0:T(8,128)S(1)} %select_maximum_fusion.2), kind=kLoop, calls=%fused_computation.8.clone.1 | loop fusion | flops 12574720 | bytes 16842752 | tf_op jit(solution)/shard_map/while/body/eval_jaxpr/reduce_sum | solution.py:89
  648.8 11.1 %fusion.69 = f32[16,512,72]{1,2,0:T(8,128)} fusion(f32[16,512,72]{1,2,0:T(8,128)} %get-tuple-element.185, f32[16,512,512]{2,1,0:T(8,128)} %get-tuple-element.170, f32[16,512]{1,0:T(8,128)S(1)} %select_maximum_fusion.2, bf16[8,512,16,72]{1,3,2,0:T(8,128)(2,1)} %get-tuple-element.197, s32[]{:T(128)} %get-tuple-element.182, ...), kind=kOutput, calls=%fused_computation.13.clone.1 | convolution fusion | flops 618332160 | bytes 22741504 | tf_op jit(solution)/shard_map/while/body/eval_jaxpr/hqk,khe->hqe/dot_general | solution.py:90
  659.9 9.7 %bitcast_reduce_fusion.2 = (f32[16,512]{1,0:T(8,128)S(1)}, f32[16,512,512]{2,1,0:T(8,128)}) fusion(bf16[512,16,72]{0,2,1:T(8,128)(2,1)} %get-tuple-element.196, bf16[8,512,16,72]{1,3,2,0:T(8,128)(2,1)} %get-tuple-element.195, s32[]{:T(128)} %get-tuple-element.182), kind=kOutput, calls=%fused_computation.5.clone.1 | convolution fusion | flops 612360192 | bytes 19169792 | tf_op jit(solution)/shard_map/while/body/eval_jaxpr/qhe,khe->hqk/dot_general | solution.py:83
  669.6 8.6 %fusion.67 = f32[16,512]{1,0:T(8,128)S(1)} fusion(f32[16,512,512]{2,1,0:T(8,128)} %get-tuple-element.170, f32[16,512]{1,0:T(8,128)S(1)} %select_maximum_fusion.2), kind=kLoop, calls=%fused_computation.8.clone.1 | loop fusion | flops 12574720 | bytes 16842752 | tf_op jit(solution)/shard_map/while/body/eval_jaxpr/reduce_sum | solution.py:89
  678.2 11.1 %fusion.69 = f32[16,512,72]{1,2,0:T(8,128)} fusion(f32[16,512,72]{1,2,0:T(8,128)} %get-tuple-element.185, f32[16,512,512]{2,1,0:T(8,128)} %get-tuple-element.170, f32[16,512]{1,0:T(8,128)S(1)} %select_maximum_fusion.2, bf16[8,512,16,72]{1,3,2,0:T(8,128)(2,1)} %get-tuple-element.197, s32[]{:T(128)} %get-tuple-element.182, ...), kind=kOutput, calls=%fused_computation.13.clone.1 | convolution fusion | flops 618332160 | bytes 22741504 | tf_op jit(solution)/shard_map/while/body/eval_jaxpr/hqk,khe->hqe/dot_general | solution.py:90
  689.3 9.7 %bitcast_reduce_fusion.2 = (f32[16,512]{1,0:T(8,128)S(1)}, f32[16,512,512]{2,1,0:T(8,128)}) fusion(bf16[512,16,72]{0,2,1:T(8,128)(2,1)} %get-tuple-element.196, bf16[8,512,16,72]{1,3,2,0:T(8,128)(2,1)} %get-tuple-element.195, s32[]{:T(128)} %get-tuple-element.182), kind=kOutput, calls=%fused_computation.5.clone.1 | convolution fusion | flops 612360192 | bytes 19169792 | tf_op jit(solution)/shard_map/while/body/eval_jaxpr/qhe,khe->hqk/dot_general | solution.py:83
  699.0 8.6 %fusion.67 = f32[16,512]{1,0:T(8,128)S(1)} fusion(f32[16,512,512]{2,1,0:T(8,128)} %get-tuple-element.170, f32[16,512]{1,0:T(8,128)S(1)} %select_maximum_fusion.2), kind=kLoop, calls=%fused_computation.8.clone.1 | loop fusion | flops 12574720 | bytes 16842752 | tf_op jit(solution)/shard_map/while/body/eval_jaxpr/reduce_sum | solution.py:89
  707.6 11.1 %fusion.69 = f32[16,512,72]{1,2,0:T(8,128)} fusion(f32[16,512,72]{1,2,0:T(8,128)} %get-tuple-element.185, f32[16,512,512]{2,1,0:T(8,128)} %get-tuple-element.170, f32[16,512]{1,0:T(8,128)S(1)} %select_maximum_fusion.2, bf16[8,512,16,72]{1,3,2,0:T(8,128)(2,1)} %get-tuple-element.197, s32[]{:T(128)} %get-tuple-element.182, ...), kind=kOutput, calls=%fused_computation.13.clone.1 | convolution fusion | flops 618332160 | bytes 22741504 | tf_op jit(solution)/shard_map/while/body/eval_jaxpr/hqk,khe->hqe/dot_general | solution.py:90
  718.7 9.7 %bitcast_reduce_fusion.2 = (f32[16,512]{1,0:T(8,128)S(1)}, f32[16,512,512]{2,1,0:T(8,128)}) fusion(bf16[512,16,72]{0,2,1:T(8,128)(2,1)} %get-tuple-element.196, bf16[8,512,16,72]{1,3,2,0:T(8,128)(2,1)} %get-tuple-element.195, s32[]{:T(128)} %get-tuple-element.182), kind=kOutput, calls=%fused_computation.5.clone.1 | convolution fusion | flops 612360192 | bytes 19169792 | tf_op jit(solution)/shard_map/while/body/eval_jaxpr/qhe,khe->hqk/dot_general | solution.py:83
  728.5 8.6 %fusion.67 = f32[16,512]{1,0:T(8,128)S(1)} fusion(f32[16,512,512]{2,1,0:T(8,128)} %get-tuple-element.170, f32[16,512]{1,0:T(8,128)S(1)} %select_maximum_fusion.2), kind=kLoop, calls=%fused_computation.8.clone.1 | loop fusion | flops 12574720 | bytes 16842752 | tf_op jit(solution)/shard_map/while/body/eval_jaxpr/reduce_sum | solution.py:89
  737.1 11.1 %fusion.69 = f32[16,512,72]{1,2,0:T(8,128)} fusion(f32[16,512,72]{1,2,0:T(8,128)} %get-tuple-element.185, f32[16,512,512]{2,1,0:T(8,128)} %get-tuple-element.170, f32[16,512]{1,0:T(8,128)S(1)} %select_maximum_fusion.2, bf16[8,512,16,72]{1,3,2,0:T(8,128)(2,1)} %get-tuple-element.197, s32[]{:T(128)} %get-tuple-element.182, ...), kind=kOutput, calls=%fused_computation.13.clone.1 | convolution fusion | flops 618332160 | bytes 22741504 | tf_op jit(solution)/shard_map/while/body/eval_jaxpr/hqk,khe->hqe/dot_general | solution.py:90
  748.1 9.7 %bitcast_reduce_fusion.2 = (f32[16,512]{1,0:T(8,128)S(1)}, f32[16,512,512]{2,1,0:T(8,128)}) fusion(bf16[512,16,72]{0,2,1:T(8,128)(2,1)} %get-tuple-element.196, bf16[8,512,16,72]{1,3,2,0:T(8,128)(2,1)} %get-tuple-element.195, s32[]{:T(128)} %get-tuple-element.182), kind=kOutput, calls=%fused_computation.5.clone.1 | convolution fusion | flops 612360192 | bytes 19169792 | tf_op jit(solution)/shard_map/while/body/eval_jaxpr/qhe,khe->hqk/dot_general | solution.py:83
  766.5 11.1 %fusion.69 = f32[16,512,72]{1,2,0:T(8,128)} fusion(f32[16,512,72]{1,2,0:T(8,128)} %get-tuple-element.185, f32[16,512,512]{2,1,0:T(8,128)} %get-tuple-element.170, f32[16,512]{1,0:T(8,128)S(1)} %select_maximum_fusion.2, bf16[8,512,16,72]{1,3,2,0:T(8,128)(2,1)} %get-tuple-element.197, s32[]{:T(128)} %get-tuple-element.182, ...), kind=kOutput, calls=%fused_computation.13.clone.1 | convolution fusion | flops 618332160 | bytes 22741504 | tf_op jit(solution)/shard_map/while/body/eval_jaxpr/hqk,khe->hqe/dot_general | solution.py:90
  (75 shorter events, 71.6 us)
Async XLA Ops:
  6.5 773.1 %copy-start = (bf16[1152,1152]{1,0:T(8,128)(2,1)S(1)}, bf16[1152,1152]{1,0:T(8,128)(2,1)}, u32[]{:S(2)}) copy-start(bf16[1152,1152]{1,0:T(8,128)(2,1)} %param.19) | copy-start | bytes 7962628
  6.5 30.5 %copy-start.1 = (bf16[128,1152]{1,0:T(8,128)(2,1)S(1)}, bf16[128,1152]{1,0:T(8,128)(2,1)}, u32[]{:S(2)}) copy-start(bf16[128,1152]{1,0:T(8,128)(2,1)} %param.15) | copy-start | bytes 884740
  44.6 38.4 %all-to-all-start.1 = ((bf16[128,6,1152]{2,1,0:T(8,128)(2,1)}), bf16[128,6,1152]{2,1,0:T(8,128)(2,1)}, u32[]{:S(2)}, u32[]{:S(2)}) async-start(bf16[128,6,1152]{2,1,0:T(8,128)(2,1)} %reshape.223), calls=%async_computation.1 | async-start | bytes 4718592 | tf_op jit(solution)/shard_map/all_to_all | solution.py:50
  49.9 247.6 %all-gather.3.cloned.1.call-start = ((), (), s32[]{:S(2)}) async-start(), calls=%async_computation.2 | async-start | bytes 10616832 | tf_op jit(solution)/shard_map/all_gather | solution.py:72
  86.9 5.4 copy-start.4
  92.3 8.0 %copy-start.2 = (bf16[1,512,1152]{2,1,0:T(8,128)(2,1)S(1)}, bf16[1,512,1152]{2,1,0:T(8,128)(2,1)}, u32[]{:S(2)}) copy-start(bf16[1,512,1152]{2,1,0:T(8,128)(2,1)} %param.11) | copy-start | bytes 3538948
  100.3 11.5 %copy-start.5 = (f32[512,3456]{1,0:T(8,128)}, f32[512,3456]{1,0:T(8,128)S(1)}, u32[]{:S(2)}) copy-start(f32[512,3456]{1,0:T(8,128)S(1)} %fusion.19) | copy-start | bytes 21233668
  113.7 374.5 %all-gather.5.cloned.1.call-start = ((), (), s32[]{:S(2)}) async-start(), calls=%async_computation.3 | async-start | bytes 10616832 | tf_op jit(solution)/shard_map/all_gather | solution.py:73
  777.6 2.1 copy-start.3
Sparse Core Ops, SparseCore 0:
  113.9 183.5 all-gather.2
  299.1 189.0 all-gather.4
where the time goes:
time: 794 us; the launch traced here: 791 us
  waiting for transfers between devices  347 us (44%)
  matrix products  190 us (24%)
  local copies, waits for them, and re-layouts  137 us (17%)
  other arithmetic  76 us (10%)
  blocking collectives  21 us (3%)
  between operations  14.2 us (2%)
    all_gather x1, waiting for transfers between devices, per_device(): keys_piece = lax.all_gather(keys_here, 'ctx', axis=0, tiled=True)  181 us
    all_gather x1, waiting for transfers between devices, per_device(): values_piece = lax.all_gather(values_here, 'ctx', axis=0, tiled=True)  136 us
    dot_general x8, matrix products, advance(): jnp.einsum('hqk,khe->hqe', expo.astype(jnp.bfloat16), value_block, prefer...  88 us
    dot_general x8, matrix products, advance(): jnp.einsum('qhe,khe->hqk', query_heads, key_block, preferred_element_type...  77.9 us
    reduce_sum x8, other arithmetic, advance(): denominator = denominator * shrink + jnp.sum(expo, axis=2)  68.4 us
    unnamed x14, local copies, waits for them, and re-layouts  43 us
    reshape x1, local copies, waits for them, and re-layouts, per_device(): values_piece.reshape(piece_rows // block_rows, block_rows, HEADS, head_dim)  33.2 us
    reshape x1, local copies, waits for them, and re-layouts, per_device(): keys_piece.reshape(piece_rows // block_rows, block_rows, HEADS, head_dim)  33.2 us
  transfers between devices with their start and end apart: 3, of which 3 were waited for; matrix products, arithmetic and copies ran while one was open for 8% of the time, Pallas kernels for 0%

commit v1 on v0

--- a/solution.py
+++ b/solution.py
@@ -5,6 +5,11 @@
 from jax.sharding import PartitionSpec as P
 
 HEADS = 16
+
+
+def launch_knots_up(point, z_in, axis_id):
+    fresh = lax.all_gather(jnp.concatenate([point, z_in], 1), axis_id, tiled=True, axis=0)
+    return jnp.split(fresh, [point.shape[1]], 1)
 
 
 def layer_modulate(device_tokens, mods, width):
@@ -69,8 +74,7 @@
         jnp.zeros((HEADS, tok_rows), jnp.float32),
         jnp.zeros((HEADS, tok_rows, head_dim), jnp.float32),
     )
-    keys_piece = lax.all_gather(keys_here, "ctx", axis=0, tiled=True)
-    values_piece = lax.all_gather(values_here, "ctx", axis=0, tiled=True)
+    keys_piece, values_piece = launch_knots_up(keys_here, values_here, "ctx")
     piece_rows = keys_piece.shape[0]
     block_rows = math.gcd(piece_rows, 512)
     key_blocks = keys_piece.reshape(piece_rows // block_rows, block_rows, HEADS, head_dim)

time: 794 us -> 851 us (1.072)
  waiting for transfers between devices: 347 us -> 385 us
  local copies, waits for them, and re-layouts: 137 us -> 156 us
    all_gather x2 -> x1, waiting for transfers between devices: 317 us -> 356 us  [launch_knots_up(): lax.all_gather(jnp.concatenate([point, z_in], 1), axis_id, tiled=True, ax...]
    split x0 -> x1, local copies, waits for them, and re-layouts: none -> 14.6 us  [launch_knots_up(): return jnp.split(fresh, [point.shape[1]], 1)]
    unnamed x14 -> x16, local copies, waits for them, and re-layouts: 43 us -> 44.7 us
  transfers between devices with their start and end apart: 3 -> 2, of which waited for: 3 -> 2; matrix products, arithmetic and copies ran while one was open for 8% -> 1% of each run, Pallas kernels for 0% -> 0%
where the time goes in v1:
time: 851 us; the launch traced here: 848 us
  waiting for transfers between devices  385 us (45%)
  matrix products  190 us (22%)
  local copies, waits for them, and re-layouts  156 us (18%)
  other arithmetic  76 us (9%)
  blocking collectives  21 us (2%)
  between operations  14.2 us (2%)
    all_gather x1, waiting for transfers between devices, launch_knots_up(): lax.all_gather(jnp.concatenate([point, z_in], 1), axis_id, tiled=True, ax...  356 us
    dot_general x8, matrix products, advance(): jnp.einsum('hqk,khe->hqe', expo.astype(jnp.bfloat16), value_block, prefer...  88.2 us
    dot_general x8, matrix products, advance(): jnp.einsum('qhe,khe->hqk', query_heads, key_block, preferred_element_type...  77.9 us
    reduce_sum x8, other arithmetic, advance(): denominator = denominator * shrink + jnp.sum(expo, axis=2)  68.4 us
    unnamed x16, local copies, waits for them, and re-layouts  44.7 us
    reshape x1, local copies, waits for them, and re-layouts, per_device(): keys_piece.reshape(piece_rows // block_rows, block_rows, HEADS, head_dim)  33.2 us
    reshape x1, local copies, waits for them, and re-layouts, per_device(): values_piece.reshape(piece_rows // block_rows, block_rows, HEADS, head_dim)  33.2 us
    all_to_all x1, waiting for transfers between devices, per_device(): lax.all_to_all(served, ('region', 'ctx'), split_axis=0, concat_axis=0, ti...  29.6 us
  transfers between devices with their start and end apart: 2, of which 2 were waited for; matrix products, arithmetic and copies ran while one was open for 1% of the time, Pallas kernels for 0%

profile of v1, /device:TPU:1, one launch (start us, length us, event | category | flops | bytes accessed | tf_op | source)
XLA Modules:
  0.0 848.2 jit_solution(14959123706047776104)
XLA Ops:
  14.5 21.0 %all_to_all.14 = s32[128,1,6]{2,1,0:T(1,128)S(1)} all-to-all(s32[128,1,6]{2,1,0:T(1,128)S(1)} %bitcast.77), channel_id=1, replica_groups=mesh['region'=16,'ctx'=8] {'region','ctx'}, dimensions={0} | all-to-all | bytes 6144 | tf_op jit(solution)/shard_map/all_to_all | solution.py:46
  53.4 29.6 %all-to-all-done.1 = bf16[128,6,1152]{2,1,0:T(8,128)(2,1)} async-done(((bf16[128,6,1152]{2,1,0:T(8,128)(2,1)}), bf16[128,6,1152]{2,1,0:T(8,128)(2,1)}, u32[]{:S(2)}, u32[]{:S(2)}) %all-to-all-start.1) | async-done | bytes 1769504 | tf_op jit(solution)/shard_map/all_to_all | solution.py:55
  100.3 11.4 %convolution_convert_fusion = bf16[512,3456]{1,0:T(8,128)(2,1)S(1)} fusion(bf16[1152,3456]{1,0:T(8,128)(2,1)} %param.18, bf16[1,512,1152]{2,1,0:T(8,128)(2,1)S(1)} %copy-done.2, f32[512,3456]{1,0:T(8,128)S(1)} %fusion.19, f32[512]{0:T(512)S(1)} %add_rsqrt_fusion, f32[512]{0:T(512)S(1)} %broadcast_multiply_fusion), kind=kOutput, calls=%fused_computation.28 | convolution fusion | flops 4082761728 | bytes 17403904 | tf_op jit(solution)/shard_map/dot_general | solution.py:65
  120.0 355.9 %all-gather.2.cloned.1.call-done = bf16[4096,2304]{1,0:T(8,128)(2,1)} async-done(((bf16[512,2304]{1,0:T(8,128)(2,1)}), bf16[4096,2304]{1,0:T(8,128)(2,1)}) %all-gather.2.cloned.1.call-update) | async-done | bytes 18874384 | tf_op jit(solution)/shard_map/all_gather | solution.py:11
  475.9 14.6 %fusion.52 = (bf16[4096,1152]{1,0:T(8,128)(2,1)}, bf16[4096,1152]{1,0:T(8,128)(2,1)}) fusion(bf16[4096,2304]{1,0:T(8,128)(2,1)} %all-gather.2.cloned.1.call-done), kind=kLoop, calls=%fused_computation.90 | loop fusion | bytes 37748736 | tf_op jit(solution)/shard_map/split | solution.py:12
  490.5 33.2 %reshape.260 = bf16[8,512,16,72]{3,2,1,0:T(8,128)(2,1)} reshape(bf16[4096,1152]{1,0:T(8,128)(2,1)} %get-tuple-element.118) | data formatting | bytes 18874368 | tf_op jit(solution)/shard_map/reshape | solution.py:80
  523.7 21.4 %copy.32 = bf16[8,512,16,72]{1,3,2,0:T(8,128)(2,1)} copy(bf16[8,512,16,72]{3,2,1,0:T(8,128)(2,1)} %reshape.260) | data formatting | bytes 18874368
  545.1 33.2 %reshape.261 = bf16[8,512,16,72]{3,2,1,0:T(8,128)(2,1)} reshape(bf16[4096,1152]{1,0:T(8,128)(2,1)} %get-tuple-element.117) | data formatting | bytes 18874368 | tf_op jit(solution)/shard_map/reshape | solution.py:81
  578.3 21.4 %copy.33 = bf16[8,512,16,72]{1,3,2,0:T(8,128)(2,1)} copy(bf16[8,512,16,72]{3,2,1,0:T(8,128)(2,1)} %reshape.261) | data formatting | bytes 18874368
  599.7 234.9 %while.15 = (s32[]{:T(128)}, f32[16,512]{1,0:T(8,128)S(1)}, f32[16,512]{1,0:T(8,128)S(1)}, f32[16,512,72]{1,2,0:T(8,128)}, bf16[8,512,16,72]{1,3,2,0:T(8,128)(2,...) while((s32[]{:T(128)}, f32[16,512]{1,0:T(8,128)S(1)}, ...), condition=%wide.region_7.8_spmd.clone, body=%wide.region_4.7_spmd.clone.sunk | while | flops 1243324416 | bytes 59114596 | solution.py:102
  599.7 9.7 %bitcast_reduce_fusion.2 = (f32[16,512]{1,0:T(8,128)S(1)}, f32[16,512,512]{2,1,0:T(8,128)}) fusion(bf16[512,16,72]{0,2,1:T(8,128)(2,1)} %get-tuple-element.195, bf16[8,512,16,72]{1,3,2,0:T(8,128)(2,1)} %get-tuple-element.194, s32[]{:T(128)} %get-tuple-element.181), kind=kOutput, calls=%fused_computation.5.clone.1 | convolution fusion | flops 612360192 | bytes 19169792 | tf_op jit(solution)/shard_map/while/body/eval_jaxpr/qhe,khe->hqk/dot_general | solution.py:87
  609.5 8.6 %fusion.67 = f32[16,512]{1,0:T(8,128)S(1)} fusion(f32[16,512,512]{2,1,0:T(8,128)} %get-tuple-element.169, f32[16,512]{1,0:T(8,128)S(1)} %select_maximum_fusion.2), kind=kLoop, calls=%fused_computation.8.clone.1 | loop fusion | flops 12574720 | bytes 16842752 | tf_op jit(solution)/shard_map/while/body/eval_jaxpr/reduce_sum | solution.py:93
  618.1 10.4 %fusion.69 = f32[16,512,72]{1,2,0:T(8,128)} fusion(f32[16,512,72]{1,2,0:T(8,128)} %get-tuple-element.184, f32[16,512,512]{2,1,0:T(8,128)} %get-tuple-element.169, f32[16,512]{1,0:T(8,128)S(1)} %select_maximum_fusion.2, bf16[8,512,16,72]{1,3,2,0:T(8,128)(2,1)} %get-tuple-element.196, s32[]{:T(128)} %get-tuple-element.181, ...), kind=kOutput, calls=%fused_computation.13.clone.1 | convolution fusion | flops 618332160 | bytes 22741504 | tf_op jit(solution)/shard_map/while/body/eval_jaxpr/hqk,khe->hqe/dot_general | solution.py:94
  628.5 9.7 %bitcast_reduce_fusion.2 = (f32[16,512]{1,0:T(8,128)S(1)}, f32[16,512,512]{2,1,0:T(8,128)}) fusion(bf16[512,16,72]{0,2,1:T(8,128)(2,1)} %get-tuple-element.195, bf16[8,512,16,72]{1,3,2,0:T(8,128)(2,1)} %get-tuple-element.194, s32[]{:T(128)} %get-tuple-element.181), kind=kOutput, calls=%fused_computation.5.clone.1 | convolution fusion | flops 612360192 | bytes 19169792 | tf_op jit(solution)/shard_map/while/body/eval_jaxpr/qhe,khe->hqk/dot_general | solution.py:87
  638.2 8.6 %fusion.67 = f32[16,512]{1,0:T(8,128)S(1)} fusion(f32[16,512,512]{2,1,0:T(8,128)} %get-tuple-element.169, f32[16,512]{1,0:T(8,128)S(1)} %select_maximum_fusion.2), kind=kLoop, calls=%fused_computation.8.clone.1 | loop fusion | flops 12574720 | bytes 16842752 | tf_op jit(solution)/shard_map/while/body/eval_jaxpr/reduce_sum | solution.py:93
  646.8 11.1 %fusion.69 = f32[16,512,72]{1,2,0:T(8,128)} fusion(f32[16,512,72]{1,2,0:T(8,128)} %get-tuple-element.184, f32[16,512,512]{2,1,0:T(8,128)} %get-tuple-element.169, f32[16,512]{1,0:T(8,128)S(1)} %select_maximum_fusion.2, bf16[8,512,16,72]{1,3,2,0:T(8,128)(2,1)} %get-tuple-element.196, s32[]{:T(128)} %get-tuple-element.181, ...), kind=kOutput, calls=%fused_computation.13.clone.1 | convolution fusion | flops 618332160 | bytes 22741504 | tf_op jit(solution)/shard_map/while/body/eval_jaxpr/hqk,khe->hqe/dot_general | solution.py:94
  657.9 9.7 %bitcast_reduce_fusion.2 = (f32[16,512]{1,0:T(8,128)S(1)}, f32[16,512,512]{2,1,0:T(8,128)}) fusion(bf16[512,16,72]{0,2,1:T(8,128)(2,1)} %get-tuple-element.195, bf16[8,512,16,72]{1,3,2,0:T(8,128)(2,1)} %get-tuple-element.194, s32[]{:T(128)} %get-tuple-element.181), kind=kOutput, calls=%fused_computation.5.clone.1 | convolution fusion | flops 612360192 | bytes 19169792 | tf_op jit(solution)/shard_map/while/body/eval_jaxpr/qhe,khe->hqk/dot_general | solution.py:87
  667.7 8.6 %fusion.67 = f32[16,512]{1,0:T(8,128)S(1)} fusion(f32[16,512,512]{2,1,0:T(8,128)} %get-tuple-element.169, f32[16,512]{1,0:T(8,128)S(1)} %select_maximum_fusion.2), kind=kLoop, calls=%fused_computation.8.clone.1 | loop fusion | flops 12574720 | bytes 16842752 | tf_op jit(solution)/shard_map/while/body/eval_jaxpr/reduce_sum | solution.py:93
  676.3 11.1 %fusion.69 = f32[16,512,72]{1,2,0:T(8,128)} fusion(f32[16,512,72]{1,2,0:T(8,128)} %get-tuple-element.184, f32[16,512,512]{2,1,0:T(8,128)} %get-tuple-element.169, f32[16,512]{1,0:T(8,128)S(1)} %select_maximum_fusion.2, bf16[8,512,16,72]{1,3,2,0:T(8,128)(2,1)} %get-tuple-element.196, s32[]{:T(128)} %get-tuple-element.181, ...), kind=kOutput, calls=%fused_computation.13.clone.1 | convolution fusion | flops 618332160 | bytes 22741504 | tf_op jit(solution)/shard_map/while/body/eval_jaxpr/hqk,khe->hqe/dot_general | solution.py:94
  687.4 9.7 %bitcast_reduce_fusion.2 = (f32[16,512]{1,0:T(8,128)S(1)}, f32[16,512,512]{2,1,0:T(8,128)}) fusion(bf16[512,16,72]{0,2,1:T(8,128)(2,1)} %get-tuple-element.195, bf16[8,512,16,72]{1,3,2,0:T(8,128)(2,1)} %get-tuple-element.194, s32[]{:T(128)} %get-tuple-element.181), kind=kOutput, calls=%fused_computation.5.clone.1 | convolution fusion | flops 612360192 | bytes 19169792 | tf_op jit(solution)/shard_map/while/body/eval_jaxpr/qhe,khe->hqk/dot_general | solution.py:87
  705.7 11.1 %fusion.69 = f32[16,512,72]{1,2,0:T(8,128)} fusion(f32[16,512,72]{1,2,0:T(8,128)} %get-tuple-element.184, f32[16,512,512]{2,1,0:T(8,128)} %get-tuple-element.169, f32[16,512]{1,0:T(8,128)S(1)} %select_maximum_fusion.2, bf16[8,512,16,72]{1,3,2,0:T(8,128)(2,1)} %get-tuple-element.196, s32[]{:T(128)} %get-tuple-element.181, ...), kind=kOutput, calls=%fused_computation.13.clone.1 | convolution fusion | flops 618332160 | bytes 22741504 | tf_op jit(solution)/shard_map/while/body/eval_jaxpr/hqk,khe->hqe/dot_general | solution.py:94
  716.8 9.7 %bitcast_reduce_fusion.2 = (f32[16,512]{1,0:T(8,128)S(1)}, f32[16,512,512]{2,1,0:T(8,128)}) fusion(bf16[512,16,72]{0,2,1:T(8,128)(2,1)} %get-tuple-element.195, bf16[8,512,16,72]{1,3,2,0:T(8,128)(2,1)} %get-tuple-element.194, s32[]{:T(128)} %get-tuple-element.181), kind=kOutput, calls=%fused_computation.5.clone.1 | convolution fusion | flops 612360192 | bytes 19169792 | tf_op jit(solution)/shard_map/while/body/eval_jaxpr/qhe,khe->hqk/dot_general | solution.py:87
  726.6 8.6 %fusion.67 = f32[16,512]{1,0:T(8,128)S(1)} fusion(f32[16,512,512]{2,1,0:T(8,128)} %get-tuple-element.169, f32[16,512]{1,0:T(8,128)S(1)} %select_maximum_fusion.2), kind=kLoop, calls=%fused_computation.8.clone.1 | loop fusion | flops 12574720 | bytes 16842752 | tf_op jit(solution)/shard_map/while/body/eval_jaxpr/reduce_sum | solution.py:93
  735.2 11.1 %fusion.69 = f32[16,512,72]{1,2,0:T(8,128)} fusion(f32[16,512,72]{1,2,0:T(8,128)} %get-tuple-element.184, f32[16,512,512]{2,1,0:T(8,128)} %get-tuple-element.169, f32[16,512]{1,0:T(8,128)S(1)} %select_maximum_fusion.2, bf16[8,512,16,72]{1,3,2,0:T(8,128)(2,1)} %get-tuple-element.196, s32[]{:T(128)} %get-tuple-element.181, ...), kind=kOutput, calls=%fused_computation.13.clone.1 | convolution fusion | flops 618332160 | bytes 22741504 | tf_op jit(solution)/shard_map/while/body/eval_jaxpr/hqk,khe->hqe/dot_general | solution.py:94
  746.3 9.7 %bitcast_reduce_fusion.2 = (f32[16,512]{1,0:T(8,128)S(1)}, f32[16,512,512]{2,1,0:T(8,128)}) fusion(bf16[512,16,72]{0,2,1:T(8,128)(2,1)} %get-tuple-element.195, bf16[8,512,16,72]{1,3,2,0:T(8,128)(2,1)} %get-tuple-element.194, s32[]{:T(128)} %get-tuple-element.181), kind=kOutput, calls=%fused_computation.5.clone.1 | convolution fusion | flops 612360192 | bytes 19169792 | tf_op jit(solution)/shard_map/while/body/eval_jaxpr/qhe,khe->hqk/dot_general | solution.py:87
  764.6 11.1 %fusion.69 = f32[16,512,72]{1,2,0:T(8,128)} fusion(f32[16,512,72]{1,2,0:T(8,128)} %get-tuple-element.184, f32[16,512,512]{2,1,0:T(8,128)} %get-tuple-element.169, f32[16,512]{1,0:T(8,128)S(1)} %select_maximum_fusion.2, bf16[8,512,16,72]{1,3,2,0:T(8,128)(2,1)} %get-tuple-element.196, s32[]{:T(128)} %get-tuple-element.181, ...), kind=kOutput, calls=%fused_computation.13.clone.1 | convolution fusion | flops 618332160 | bytes 22741504 | tf_op jit(solution)/shard_map/while/body/eval_jaxpr/hqk,khe->hqe/dot_general | solution.py:94
  775.7 9.7 %bitcast_reduce_fusion.2 = (f32[16,512]{1,0:T(8,128)S(1)}, f32[16,512,512]{2,1,0:T(8,128)}) fusion(bf16[512,16,72]{0,2,1:T(8,128)(2,1)} %get-tuple-element.195, bf16[8,512,16,72]{1,3,2,0:T(8,128)(2,1)} %get-tuple-element.194, s32[]{:T(128)} %get-tuple-element.181), kind=kOutput, calls=%fused_computation.5.clone.1 | convolution fusion | flops 612360192 | bytes 19169792 | tf_op jit(solution)/shard_map/while/body/eval_jaxpr/qhe,khe->hqk/dot_general | solution.py:87
  785.5 8.6 %fusion.67 = f32[16,512]{1,0:T(8,128)S(1)} fusion(f32[16,512,512]{2,1,0:T(8,128)} %get-tuple-element.169, f32[16,512]{1,0:T(8,128)S(1)} %select_maximum_fusion.2), kind=kLoop, calls=%fused_computation.8.clone.1 | loop fusion | flops 12574720 | bytes 16842752 | tf_op jit(solution)/shard_map/while/body/eval_jaxpr/reduce_sum | solution.py:93
  794.1 11.1 %fusion.69 = f32[16,512,72]{1,2,0:T(8,128)} fusion(f32[16,512,72]{1,2,0:T(8,128)} %get-tuple-element.184, f32[16,512,512]{2,1,0:T(8,128)} %get-tuple-element.169, f32[16,512]{1,0:T(8,128)S(1)} %select_maximum_fusion.2, bf16[8,512,16,72]{1,3,2,0:T(8,128)(2,1)} %get-tuple-element.196, s32[]{:T(128)} %get-tuple-element.181, ...), kind=kOutput, calls=%fused_computation.13.clone.1 | convolution fusion | flops 618332160 | bytes 22741504 | tf_op jit(solution)/shard_map/while/body/eval_jaxpr/hqk,khe->hqe/dot_general | solution.py:94
  805.2 9.7 %bitcast_reduce_fusion.2 = (f32[16,512]{1,0:T(8,128)S(1)}, f32[16,512,512]{2,1,0:T(8,128)}) fusion(bf16[512,16,72]{0,2,1:T(8,128)(2,1)} %get-tuple-element.195, bf16[8,512,16,72]{1,3,2,0:T(8,128)(2,1)} %get-tuple-element.194, s32[]{:T(128)} %get-tuple-element.181), kind=kOutput, calls=%fused_computation.5.clone.1 | convolution fusion | flops 612360192 | bytes 19169792 | tf_op jit(solution)/shard_map/while/body/eval_jaxpr/qhe,khe->hqk/dot_general | solution.py:87
  814.9 8.6 %fusion.67 = f32[16,512]{1,0:T(8,128)S(1)} fusion(f32[16,512,512]{2,1,0:T(8,128)} %get-tuple-element.169, f32[16,512]{1,0:T(8,128)S(1)} %select_maximum_fusion.2), kind=kLoop, calls=%fused_computation.8.clone.1 | loop fusion | flops 12574720 | bytes 16842752 | tf_op jit(solution)/shard_map/while/body/eval_jaxpr/reduce_sum | solution.py:93
  823.5 11.1 %fusion.69 = f32[16,512,72]{1,2,0:T(8,128)} fusion(f32[16,512,72]{1,2,0:T(8,128)} %get-tuple-element.184, f32[16,512,512]{2,1,0:T(8,128)} %get-tuple-element.169, f32[16,512]{1,0:T(8,128)S(1)} %select_maximum_fusion.2, bf16[8,512,16,72]{1,3,2,0:T(8,128)(2,1)} %get-tuple-element.196, s32[]{:T(128)} %get-tuple-element.181, ...), kind=kOutput, calls=%fused_computation.13.clone.1 | convolution fusion | flops 618332160 | bytes 22741504 | tf_op jit(solution)/shard_map/while/body/eval_jaxpr/hqk,khe->hqe/dot_general | solution.py:94
  (76 shorter events, 74.7 us)
Async XLA Ops:
  6.5 830.2 %copy-start = (bf16[1152,1152]{1,0:T(8,128)(2,1)S(1)}, bf16[1152,1152]{1,0:T(8,128)(2,1)}, u32[]{:S(2)}) copy-start(bf16[1152,1152]{1,0:T(8,128)(2,1)} %param.19) | copy-start | bytes 7962628
  6.5 30.5 %copy-start.1 = (bf16[128,1152]{1,0:T(8,128)(2,1)S(1)}, bf16[128,1152]{1,0:T(8,128)(2,1)}, u32[]{:S(2)}) copy-start(bf16[128,1152]{1,0:T(8,128)(2,1)} %param.15) | copy-start | bytes 884740
  44.6 38.4 %all-to-all-start.1 = ((bf16[128,6,1152]{2,1,0:T(8,128)(2,1)}), bf16[128,6,1152]{2,1,0:T(8,128)(2,1)}, u32[]{:S(2)}, u32[]{:S(2)}) async-start(bf16[128,6,1152]{2,1,0:T(8,128)(2,1)} %reshape.223), calls=%async_computation.1 | async-start | bytes 4718592 | tf_op jit(solution)/shard_map/all_to_all | solution.py:55
  49.9 426.0 %all-gather.2.cloned.1.call-start = ((), (), s32[]{:S(2)}) async-start(), calls=%async_computation.2 | async-start | bytes 21233664 | tf_op jit(solution)/shard_map/all_gather | solution.py:11
  86.9 5.4 copy-start.5
  92.3 8.0 copy-start.2
  100.3 11.5 %copy-start.6 = (f32[512,3456]{1,0:T(8,128)}, f32[512,3456]{1,0:T(8,128)S(1)}, u32[]{:S(2)}) copy-start(f32[512,3456]{1,0:T(8,128)S(1)} %fusion.19) | copy-start | bytes 21233668
  111.8 1.8 copy-start.4
  834.6 2.1 copy-start.3
Sparse Core Ops, SparseCore 0:
  115.3 360.5 all-gather.1
